TPU v7x, 128 devices: a whole 4x4x4 slice. The times are simulated.
128 devices in a mesh: grp: 16 (over z, y), tok: 8 (over x, core).
Axes of the slice: x: 4, y: 4, z: 4, core: 2. Of those that a mesh axis runs over, the one named last changes fastest.
Arguments:
- queries: bfloat16 [16384, 5120], P(('grp', 'tok')), may hold values from -6 to 6
- rotated_keys_values: bfloat16 [16384, 2048], P(('grp', 'tok')), may hold values from -6 to 6
- prompt_window_index: int32 [16, 1024], P('grp', 'tok'), may hold values from 0 to 1, never falling along the last dimension, each value on 1 to 768 neighbouring positions
- residual: bfloat16 [16384, 5120], P(('grp', 'tok')), may hold values from -8 to 8
- ffn_gain: float32 [5120], replicated, may hold values from 0.1 to 1.9
- gate_weight: bfloat16 [5120, 8192], P(None, 'grp'), may hold values from -0.078125 to 0.078125
- up_weight: bfloat16 [5120, 8192], P(None, 'grp'), may hold values from -0.078125 to 0.078125
- paged_cache: bfloat16 [2048, 16, 2048], P(('grp', 'tok')), may hold values from -6 to 6
- page_table: int32 [16, 128], P('grp'), may hold values from 0 to 127, each once within a row
Outputs:
- attended: bfloat16 [16384, 5120], P(('grp', 'tok'))
- hidden: bfloat16 [16384, 8192], P(('grp', 'tok'))
- cache_out: bfloat16 [2048, 16, 2048], P(('grp', 'tok'))
All inputs are finite; a program needn't handle non-finite values.
Results may differ from a plain program's by a relative error of at most 0.012.
Values may be sent and summed in bfloat16 or wider, within the bound.
A program may use at most 128 MiB of HBM per device.

v0:
```python
import math
import jax
import jax.numpy as jnp
from jax import lax
from jax.sharding import PartitionSpec as P

QUERY_HEADS = 40
KEY_VALUE_HEADS = 8
HEAD_SIZE = 128
PAGE_TOKENS = 16
MASK_FILLER = -1e30


def on_device(
    queries,
    rotated_keys_values,
    prompt_window_index,
    residual,
    ffn_gain,
    gate_weight,
    up_weight,
    paged_cache,
    page_table,
):
    count_of_rows = queries.shape[0]
    kv_width = rotated_keys_values.shape[1]
    group_split = QUERY_HEADS // KEY_VALUE_HEADS
    slot_count = paged_cache.shape[0]
    tok_index = lax.axis_index("tok")
    first_row = tok_index * count_of_rows
    grouped_rows = queries.reshape(count_of_rows, KEY_VALUE_HEADS, group_split, HEAD_SIZE)
    own_segment = prompt_window_index[0]
    own_place = first_row + jnp.arange(count_of_rows)
    slot_table = page_table[0]
    score_scale = 1.0 / math.sqrt(HEAD_SIZE)
    initial = (
        jnp.full((count_of_rows, KEY_VALUE_HEADS, group_split), MASK_FILLER, jnp.float32),
        jnp.zeros((count_of_rows, KEY_VALUE_HEADS, group_split), jnp.float32),
        jnp.zeros((count_of_rows, KEY_VALUE_HEADS, group_split, HEAD_SIZE), jnp.float32),
        paged_cache,
    )
    key_value_portion = lax.all_gather(rotated_keys_values, "tok", axis=0, tiled=True)
    seg_piece = lax.all_gather(own_segment, "tok", axis=0, tiled=True)
    count_of_keys = key_value_portion.shape[0]
    rows_of_keys = key_value_portion[:, : KEY_VALUE_HEADS * HEAD_SIZE].reshape(
        count_of_keys, KEY_VALUE_HEADS, HEAD_SIZE
    )
    rows_of_values = key_value_portion[:, KEY_VALUE_HEADS * HEAD_SIZE :].reshape(
        count_of_keys, KEY_VALUE_HEADS, HEAD_SIZE
    )
    key_place = jnp.arange(count_of_keys)
    live_mask = (seg_piece[None, :] == own_segment[:, None]) & (
        key_place[None, :] <= own_place[:, None]
    )
    running = (initial[0], initial[1], initial[2])
    run_max, run_sum, partial_value = running
    scores = (
        jnp.einsum("qgrd,kgd->qgrk", grouped_rows, rows_of_keys, preferred_element_type=jnp.float32)
        * score_scale
    )
    scores = jnp.where(live_mask[:, None, None, :], scores, MASK_FILLER)
    new_max = jnp.maximum(run_max, jnp.max(scores, axis=-1))
    weights = jnp.where(live_mask[:, None, None, :], jnp.exp(scores - new_max[..., None]), 0.0)
    run_sum = jnp.sum(weights, axis=-1)
    partial_value = jnp.einsum(
        "qgrk,kgd->qgrd",
        weights.astype(jnp.bfloat16),
        rows_of_values,
        preferred_element_type=jnp.float32,
    )
    running = (new_max, run_sum, partial_value)
    page_count = count_of_keys // PAGE_TOKENS
    targets = (
        lax.dynamic_slice_in_dim(slot_table, jnp.int32(0) // PAGE_TOKENS, page_count)
        - tok_index * slot_count
    )
    onehot = targets[None, :] == jnp.arange(slot_count)[:, None]
    placed = jnp.dot(
        onehot.astype(jnp.bfloat16),
        key_value_portion.reshape(page_count, PAGE_TOKENS * kv_width),
        preferred_element_type=jnp.float32,
    )
    placed = placed.astype(jnp.bfloat16).reshape(slot_count, PAGE_TOKENS, kv_width)
    written = jnp.where(jnp.any(onehot, axis=1)[:, None, None], placed, initial[3])
    run_sum = running[1]
    partial_value = running[2]
    attention = (
        (partial_value / run_sum[..., None])
        .reshape(count_of_rows, QUERY_HEADS * HEAD_SIZE)
        .astype(jnp.bfloat16)
    )
    attended = (residual.astype(jnp.float32) + attention.astype(jnp.float32)).astype(jnp.bfloat16)
    widened = attended.astype(jnp.float32)
    normed = (
        widened * lax.rsqrt(jnp.mean(widened * widened, axis=-1, keepdims=True) + 1e-06) * ffn_gain
    ).astype(jnp.bfloat16)
    tok_count = lax.axis_size("tok")
    grp_count = lax.axis_size("grp")
    col_width = gate_weight.shape[1] // tok_count
    gate_cols = lax.dynamic_slice_in_dim(gate_weight, tok_index * col_width, col_width, 1)
    up_cols = lax.dynamic_slice_in_dim(up_weight, tok_index * col_width, col_width, 1)
    gate_all, up_all = (
        lax.all_gather(gate_cols, "grp", axis=1, tiled=True),
        lax.all_gather(up_cols, "grp", axis=1, tiled=True),
    )
    shards = lax.all_gather(normed, "tok", axis=0, tiled=True)
    gate_sum = jnp.dot(shards, gate_all, preferred_element_type=jnp.float32)
    up_sum = jnp.dot(shards, up_all, preferred_element_type=jnp.float32)
    produced = (jax.nn.silu(gate_sum) * up_sum).astype(jnp.bfloat16)
    returned = lax.all_to_all(produced, "tok", split_axis=0, concat_axis=1, tiled=True)
    hidden = (
        returned.reshape(count_of_rows, tok_count, grp_count, col_width)
        .transpose(0, 2, 1, 3)
        .reshape(count_of_rows, tok_count * grp_count * col_width)
    )
    return (attended, hidden, written)


def solution(mesh):
    in_specs = (
        P(("grp", "tok"), None),
        P(("grp", "tok"), None),
        P("grp", "tok"),
        P(("grp", "tok"), None),
        P(),
        P(None, "grp"),
        P(None, "grp"),
        P(("grp", "tok"), None, None),
        P("grp", None),
    )
    out_specs = (P(("grp", "tok"), None), P(("grp", "tok"), None), P(("grp", "tok"), None, None))
    return jax.shard_map(
        on_device, mesh=mesh, in_specs=in_specs, out_specs=out_specs, check_vma=False
    )
```

profile of v0, /device:TPU:1, one launch (start us, length us, event | category | flops | bytes accessed | tf_op | source)
XLA Modules:
  0.0 340.2 jit_solution(3943348926296142948)
XLA Ops:
  7.2 2.1 copy.48
  14.0 11.8 %all-gather = s32[1,1024]{1,0:T(1,128)S(1)} all-gather(s32[1,128]{1,0:T(1,128)S(1)} %copy-done.6), channel_id=2, replica_groups=mesh['grp'=16,'tok'=8] {'tok'}, dimensions={1}, use_global_device_ids=true | all-gather | bytes 4608 | tf_op jit(solution)/shard_map/all_gather | solution.py:43
  26.0 23.9 %all-gather.6.cloned.1.call-done = bf16[1024,2048]{0,1:T(8,128)(2,1)} async-done(((bf16[128,2048]{0,1:T(8,128)(2,1)}), bf16[1024,2048]{0,1:T(8,128)(2,1)}) %all-gather.6.cloned.1.call-update) | async-done | bytes 4194320 | tf_op jit(solution)/shard_map/all_gather | solution.py:42
  50.0 4.0 %fusion.18 = (bf16[1024,1024]{0,1:T(8,128)(2,1)S(1)}, bf16[1024,1024]{0,1:T(8,128)(2,1)}) fusion(bf16[1024,2048]{0,1:T(8,128)(2,1)} %all-gather.6.cloned.1.call-done), kind=kLoop, calls=%fused_computation.33 | loop fusion | bytes 8388608 | tf_op jit(solution)/shard_map/slice | solution.py:45
  53.9 4.6 %fusion = (f32[128,8,5]{0,2,1:T(8,128)S(1)}, f32[8,1024,128,5]{2,1,3,0:T(8,128)S(1)}) fusion(pred[128,1024]{0,1:T(8,128)(4,1)S(1)} %fusion.12, bf16[1024,8,128,1]{0,2,3,1:T(8,128)(2,1)S(1)} %bitcast.53, bf16[128,8,5,128]{0,3,2,1:T(8,128)(2,1)} %bitcast.56), kind=kOutput, calls=%fused_computation.3 | convolution fusion | flops 1357900800 | bytes 24530944 | tf_op jit(solution)/shard_map/qgrd,kgd->qgrk/dot_general | solution.py:58
  58.6 5.0 %fusion.1 = f32[128,8,5]{0,2,1:T(8,128)S(1)} fusion(f32[8,1024,128,5]{2,1,3,0:T(8,128)S(1)} %get-tuple-element.20, f32[128,8,5]{0,2,1:T(8,128)S(1)} %broadcast_maximum_fusion, pred[128,1024]{0,1:T(8,128)(4,1)S(1)} %fusion.12), kind=kLoop, calls=%fused_computation.4 | loop fusion | flops 26209280 | bytes 21143552 | tf_op jit(solution)/shard_map/reduce_sum | solution.py:64
  63.6 3.3 copy-done
  67.0 10.3 %fusion.9 = bf16[128,8,5,128]{0,3,2,1:T(8,128)(2,1)S(1)} fusion(bf16[1024,8,128,1]{0,2,3,1:T(8,128)(2,1)S(1)} %bitcast.59, f32[8,1024,128,5]{2,1,3,0:T(8,128)} %copy-done, f32[128,8,5]{0,2,1:T(8,128)S(1)} %broadcast_maximum_fusion, pred[128,1024]{0,1:T(8,128)(4,1)S(1)} %fusion.12, f32[128,8,5]{0,2,1:T(8,128)S(1)} %fusion.1), kind=kOutput, calls=%fused_computation.15 | convolution fusion | flops 1369702400 | bytes 24551424 | tf_op jit(solution)/shard_map/qgrk,kgd->qgrd/dot_general | solution.py:65
  77.2 1.8 bitcast_convert_fusion
  79.0 2.2 copy.53
  81.1 1.8 fusion.6
  85.7 1.8 constant_dynamic-slice_fusion
  88.8 45.0 %all-gather.10.cloned.1.call-done = bf16[5120,1024]{0,1:T(8,128)(2,1)} async-done(((bf16[5120,64]{0,1:T(8,128)(2,1)}), bf16[5120,1024]{0,1:T(8,128)(2,1)}) %all-gather.10.cloned.1.call-update) | async-done | bytes 10485776 | tf_op jit(solution)/shard_map/all_gather | solution.py:103
  133.8 60.8 %all-gather.8.cloned.1.call-done = bf16[1024,5120]{1,0:T(8,128)(2,1)} async-done(((bf16[128,5120]{1,0:T(8,128)(2,1)}), bf16[1024,5120]{1,0:T(8,128)(2,1)}) %all-gather.8.cloned.1.call-update) | async-done | bytes 10485776 | tf_op jit(solution)/shard_map/all_gather | solution.py:106
  194.6 17.3 %fusion.19 = f32[1024,1024]{1,0:T(8,128)} fusion(bf16[1024,5120]{1,0:T(8,128)(2,1)} %all-gather.8.cloned.1.call-done, bf16[5120,1024]{0,1:T(8,128)(2,1)} %all-gather.10.cloned.1.call-done), kind=kOutput, calls=%fused_computation.34 | convolution fusion | flops 10737418240 | bytes 25165824 | tf_op jit(solution)/shard_map/dot_general | solution.py:107
  211.9 65.2 %all-gather.12.cloned.1.call-done = bf16[5120,1024]{0,1:T(8,128)(2,1)} async-done(((bf16[5120,64]{0,1:T(8,128)(2,1)}), bf16[5120,1024]{0,1:T(8,128)(2,1)}) %all-gather.12.cloned.1.call-update) | async-done | bytes 10485776 | tf_op jit(solution)/shard_map/all_gather | solution.py:104
  277.0 17.3 %multiply_convert_fusion = bf16[1024,1024]{1,0:T(8,128)(2,1)S(1)} fusion(f32[1024,1024]{1,0:T(8,128)} %fusion.19, bf16[1024,5120]{1,0:T(8,128)(2,1)} %all-gather.8.cloned.1.call-done, bf16[5120,1024]{0,1:T(8,128)(2,1)} %all-gather.12.cloned.1.call-done), kind=kOutput, calls=%fused_computation.8 | convolution fusion | flops 10743709696 | bytes 27262976 | tf_op jit(solution)/shard_map/dot_general | solution.py:108
  294.4 2.4 copy.56
  296.7 4.9 %all-to-all-start = ((bf16[8,128,1024]{1,2,0:T(8,128)(2,1)}), bf16[8,128,1024]{1,2,0:T(8,128)(2,1)S(1)}, u32[]{:S(2)}, u32[]{:S(2)}) async-start(bf16[8,128,1024]{1,2,0:T(8,128)(2,1)} %copy.56), calls=%async_computation | async-start | bytes 4194304 | tf_op jit(solution)/shard_map/all_to_all | solution.py:110
  301.8 6.5 %copy.58 = bf16[1024,2048]{1,0:T(8,128)(2,1)} copy(bf16[1024,2048]{0,1:T(8,128)(2,1)} %all-gather.6.cloned.1.call-done) | data formatting | bytes 8388608 | tf_op jit(solution)/shard_map/all_gather | solution.py:42
  308.3 7.5 %reshape.103 = bf16[64,32768]{1,0:T(8,128)(2,1)} reshape(bf16[1024,2048]{1,0:T(8,128)(2,1)} %copy.58) | data formatting | bytes 8388608 | tf_op jit(solution)/shard_map/reshape | solution.py:80
  315.7 2.9 convolution_convert_fusion
  320.4 7.6 %all-to-all-done = bf16[8,128,1024]{1,2,0:T(8,128)(2,1)S(1)} async-done(((bf16[8,128,1024]{1,2,0:T(8,128)(2,1)}), bf16[8,128,1024]{1,2,0:T(8,128)(2,1)S(1)}, u32[]{:S(2)}, u32[]{:S(2)}) %all-to-all-start) | async-done | bytes 2097184 | tf_op jit(solution)/shard_map/all_to_all | solution.py:110
  329.6 4.1 %copy.59 = bf16[128,8192]{1,0:T(8,128)(2,1)} copy(bf16[128,8192]{0,1:T(8,128)(2,1)} %bitcast.55) | data formatting | bytes 4194304
  (37 shorter events, 12.4 us)
Async XLA Ops:
  7.2 5.4 %copy-start.3 = (bf16[128,5120]{1,0:T(8,128)(2,1)S(1)}, bf16[128,5120]{1,0:T(8,128)(2,1)}, u32[]{:S(2)}) copy-start(bf16[128,5120]{1,0:T(8,128)(2,1)} %param.9) | copy-start | bytes 3932164
  7.2 42.8 %all-gather.6.cloned.1.call-start = ((), (), s32[]{:S(2)}) async-start(), calls=%async_computation.1 | async-start | bytes 4718592 | tf_op jit(solution)/shard_map/all_gather | solution.py:42
  9.4 4.7 %copy-start.6 = (s32[1,128]{1,0:T(1,128)S(1)}, s32[1,128]{1,0:T(1,128)}, u32[]{:S(2)}) copy-start(s32[1,128]{1,0:T(1,128)} %param.11) | copy-start | bytes 1540
  9.4 124.4 %all-gather.10.cloned.1.call-start = ((), (), s32[]{:S(2)}) async-start(), calls=%async_computation.3 | async-start | bytes 11141120 | tf_op jit(solution)/shard_map/all_gather | solution.py:103
  12.5 182.1 %all-gather.8.cloned.1.call-start = ((), (), s32[]{:S(2)}) async-start(), calls=%async_computation.2 | async-start | bytes 11796480 | tf_op jit(solution)/shard_map/all_gather | solution.py:106
  58.6 8.4 %copy-start = (f32[8,1024,128,5]{2,1,3,0:T(8,128)}, f32[8,1024,128,5]{2,1,3,0:T(8,128)S(1)}, u32[]{:S(2)}) copy-start(f32[8,1024,128,5]{2,1,3,0:T(8,128)S(1)} %get-tuple-element.20) | copy-start | bytes 62914564
  58.6 8.3 %copy-start.2 = (bf16[1024,1024]{0,1:T(8,128)(2,1)S(1)}, bf16[1024,1024]{0,1:T(8,128)(2,1)}, u32[]{:S(2)}) copy-start(bf16[1024,1024]{0,1:T(8,128)(2,1)} %get-tuple-element.18) | copy-start | bytes 6291460
  79.0 5.0 %copy-start.5 = (f32[5120]{0:T(1024)S(1)}, f32[5120]{0:T(1024)}, u32[]{:S(2)}) copy-start(f32[5120]{0:T(1024)} %param.13) | copy-start | bytes 61444
  82.9 1.1 copy-start.1
  85.5 191.5 %all-gather.12.cloned.1.call-start = ((), (), s32[]{:S(2)}) async-start(), calls=%async_computation.4 | async-start | bytes 11141120 | tf_op jit(solution)/shard_map/all_gather | solution.py:104
  294.3 7.3 %copy-start.7 = (s32[1,128]{1,0:T(1,128)S(1)}, s32[1,128]{1,0:T(1,128)}, u32[]{:S(2)}) copy-start(s32[1,128]{1,0:T(1,128)} %param.17) | copy-start | bytes 1540
  296.7 31.3 %all-to-all-start = ((bf16[8,128,1024]{1,2,0:T(8,128)(2,1)}), bf16[8,128,1024]{1,2,0:T(8,128)(2,1)S(1)}, u32[]{:S(2)}, u32[]{:S(2)}) async-start(bf16[8,128,1024]{1,2,0:T(8,128)(2,1)} %copy.56), calls=%async_computation | async-start | bytes 4194304 | tf_op jit(solution)/shard_map/all_to_all | solution.py:110
  315.7 3.5 %copy-start.4 = (bf16[16,16,2048]{2,1,0:T(8,128)(2,1)S(1)}, bf16[16,16,2048]{2,1,0:T(8,128)(2,1)}, u32[]{:S(2)}) copy-start(bf16[16,16,2048]{2,1,0:T(8,128)(2,1)} %param.16) | copy-start | bytes 3145732
Sparse Core Ops, SparseCore 0:
  10.3 39.6 all-gather.5
  52.7 81.0 all-gather.9
  136.1 58.4 all-gather.7
  196.6 80.4 all-gather.11
where the time goes:
time: 341 us; the launch traced here: 340 us
  waiting for transfers between devices  203 us (60%)
  matrix products  52.4 us (15%)
  local copies, waits for them, and re-layouts  42.8 us (13%)
  between operations  13.9 us (4%)
  blocking collectives  11.8 us (3%)
  other arithmetic  11.5 us (3%)
  starting transfers between devices  5.28 us (2%)
    all_gather x1, waiting for transfers between devices, on_device(): lax.all_gather(up_cols, 'grp', axis=1, tiled=True)  65.2 us
    all_gather x1, waiting for transfers between devices, on_device(): shards = lax.all_gather(normed, 'tok', axis=0, tiled=True)  60.8 us
    all_gather x1, waiting for transfers between devices, on_device(): lax.all_gather(gate_cols, 'grp', axis=1, tiled=True)  45 us
    all_gather x1, waiting for transfers between devices, on_device(): lax.all_gather(rotated_keys_values, 'tok', axis=0, tiled=True)  23.9 us
    dot_general x1, matrix products, on_device(): up_sum = jnp.dot(shards, up_all, preferred_element_type=jnp.float32)  17.3 us
    dot_general x1, matrix products, on_device(): gate_sum = jnp.dot(shards, gate_all, preferred_element_type=jnp.float32)  17.3 us
    unnamed x22, local copies, waits for them, and re-layouts  15.2 us
    all_gather x1, blocking collectives, on_device(): seg_piece = lax.all_gather(own_segment, 'tok', axis=0, tiled=True)  11.8 us
  transfers between devices with their start and end apart: 5, of which 5 were waited for; matrix products, arithmetic and copies ran while one was open for 22% of the time, Pallas kernels for 0%

commit v1 on v0

--- a/solution.py
+++ b/solution.py
@@ -9,6 +9,28 @@
 HEAD_SIZE = 128
 PAGE_TOKENS = 16
 MASK_FILLER = -1e30
+
+
+def laid_out(tiles, dim):
+    shape = list(tiles.shape[1:])
+    shape[dim] *= tiles.shape[0]
+    return jnp.moveaxis(tiles, 0, dim).reshape(shape)
+
+
+def gather_around(shard, axis, dim):
+    devices = lax.axis_size(axis)
+    pairs = [(i, (i + 1) % devices) for i in range(devices)]
+    back = [(b, a) for a, b in pairs]
+    lower, upper = ([], [])
+    for lap in range(devices - 1):
+        if lap % 2 == 0:
+            lower.append(lax.ppermute(lower[-1] if lower else shard, axis, pairs))
+        else:
+            upper.append(lax.ppermute(upper[-1] if upper else shard, axis, back))
+    blocks = jnp.stack([*lower[::-1], shard, *upper])
+    shift = lax.axis_index(axis) - len(lower)
+    blocks = blocks[(jnp.arange(devices) - shift) % devices]
+    return laid_out(blocks, dim)
 
 
 def on_device(
@@ -103,7 +125,7 @@
         lax.all_gather(gate_cols, "grp", axis=1, tiled=True),
         lax.all_gather(up_cols, "grp", axis=1, tiled=True),
     )
-    shards = lax.all_gather(normed, "tok", axis=0, tiled=True)
+    shards = gather_around(normed, "tok", 0)
     gate_sum = jnp.dot(shards, gate_all, preferred_element_type=jnp.float32)
     up_sum = jnp.dot(shards, up_all, preferred_element_type=jnp.float32)
     produced = (jax.nn.silu(gate_sum) * up_sum).astype(jnp.bfloat16)

time: 341 us -> 280 us (0.82)
  waiting for transfers between devices: 203 us -> 106 us
  local copies, waits for them, and re-layouts: 42.8 us -> 65.7 us
  starting transfers between devices: 5.28 us -> 18.1 us
    all_gather x1 -> x0, waiting for transfers between devices: 60.8 us -> none  [on_device(): shards = lax.all_gather(normed, 'tok', axis=0, tiled=True)]
    ppermute x0 -> x7, waiting for transfers between devices: none -> 54 us  [the longest x4 53.5 us: gather_around(): lower.append(lax.ppermute(lower[-1] if lower else shard, axis, pairs))]
    all_gather x1, waiting for transfers between devices: 45 us -> 0.01 us  [on_device(): lax.all_gather(gate_cols, 'grp', axis=1, tiled=True)]
    all_gather x1, waiting for transfers between devices: 65.2 us -> 23.3 us  [on_device(): lax.all_gather(up_cols, 'grp', axis=1, tiled=True)]
    ppermute x0 -> x7, starting transfers between devices: none -> 13.1 us  [the longest x4 8.56 us: gather_around(): lower.append(lax.ppermute(lower[-1] if lower else shard, axis, pairs))]
    unnamed x22 -> x32, local copies, waits for them, and re-layouts: 15.2 us -> 27.4 us
    gather x0 -> x1, local copies, waits for them, and re-layouts: none -> 9.64 us  [gather_around(): blocks = blocks[(jnp.arange(devices) - shift) % devices]]
  transfers between devices with their start and end apart: 5 -> 11, of which waited for: 5 -> 8; matrix products, arithmetic and copies ran while one was open for 22% -> 35% of each run, Pallas kernels for 0% -> 0%
where the time goes in v1:
time: 280 us; the launch traced here: 279 us
  waiting for transfers between devices  106 us (38%)
  local copies, waits for them, and re-layouts  65.7 us (23%)
  matrix products  52.7 us (19%)
  starting transfers between devices  18.1 us (6%)
  between operations  14 us (5%)
  blocking collectives  11.8 us (4%)
  other arithmetic  11.2 us (4%)
    ppermute x4, waiting for transfers between devices, gather_around(): lower.append(lax.ppermute(lower[-1] if lower else shard, axis, pairs))  53.5 us
    unnamed x32, local copies, waits for them, and re-layouts  27.4 us
    all_gather x1, waiting for transfers between devices, on_device(): lax.all_gather(up_cols, 'grp', axis=1, tiled=True)  23.3 us
    all_gather x1, waiting for transfers between devices, on_device(): lax.all_gather(rotated_keys_values, 'tok', axis=0, tiled=True)  20.9 us
    dot_general x1, matrix products, on_device(): gate_sum = jnp.dot(shards, gate_all, preferred_element_type=jnp.float32)  17.5 us
    dot_general x1, matrix products, on_device(): up_sum = jnp.dot(shards, up_all, preferred_element_type=jnp.float32)  17.3 us
    all_gather x1, blocking collectives, on_device(): seg_piece = lax.all_gather(own_segment, 'tok', axis=0, tiled=True)  11.8 us
    dot_general x1, matrix products, on_device(): jnp.einsum('qgrk,kgd->qgrd', weights.astype(jnp.bfloat16), rows_of_values...  10.3 us
  transfers between devices with their start and end apart: 11, of which 8 were waited for; matrix products, arithmetic and copies ran while one was open for 35% of the time, Pallas kernels for 0%

profile of v1, /device:TPU:1, one launch (start us, length us, event | category | flops | bytes accessed | tf_op | source)
XLA Modules:
  0.0 279.2 jit_solution(287303565148200076)
XLA Ops:
  15.6 11.8 %all-gather = s32[1,1024]{1,0:T(1,128)S(1)} all-gather(s32[1,128]{1,0:T(1,128)S(1)} %copy-done.8), channel_id=2, replica_groups=mesh['grp'=16,'tok'=8] {'tok'}, dimensions={1}, use_global_device_ids=true | all-gather | bytes 4608 | tf_op jit(solution)/shard_map/all_gather | solution.py:65
  29.0 20.9 %all-gather.5.cloned.1.call-done = bf16[1024,2048]{0,1:T(8,128)(2,1)} async-done(((bf16[128,2048]{0,1:T(8,128)(2,1)}), bf16[1024,2048]{0,1:T(8,128)(2,1)}) %all-gather.5.cloned.1.call-update) | async-done | bytes 4194320 | tf_op jit(solution)/shard_map/all_gather | solution.py:64
  49.9 4.0 %fusion.20 = (bf16[1024,1024]{0,1:T(8,128)(2,1)S(1)}, bf16[1024,1024]{0,1:T(8,128)(2,1)}) fusion(bf16[1024,2048]{0,1:T(8,128)(2,1)} %all-gather.5.cloned.1.call-done), kind=kLoop, calls=%fused_computation.49 | loop fusion | bytes 8388608 | tf_op jit(solution)/shard_map/slice | solution.py:67
  53.9 4.6 %fusion = (f32[128,8,5]{0,2,1:T(8,128)S(1)}, f32[8,1024,128,5]{2,1,3,0:T(8,128)S(1)}) fusion(pred[128,1024]{0,1:T(8,128)(4,1)S(1)} %fusion.12, bf16[1024,8,128,1]{0,2,3,1:T(8,128)(2,1)S(1)} %bitcast.72, bf16[128,8,5,128]{0,3,2,1:T(8,128)(2,1)} %bitcast.77), kind=kOutput, calls=%fused_computation.4 | convolution fusion | flops 1357900800 | bytes 24530944 | tf_op jit(solution)/shard_map/qgrd,kgd->qgrk/dot_general | solution.py:80
  58.6 5.0 %fusion.1 = f32[128,8,5]{0,2,1:T(8,128)S(1)} fusion(f32[8,1024,128,5]{2,1,3,0:T(8,128)S(1)} %get-tuple-element.20, f32[128,8,5]{0,2,1:T(8,128)S(1)} %broadcast_maximum_fusion, pred[128,1024]{0,1:T(8,128)(4,1)S(1)} %fusion.12), kind=kLoop, calls=%fused_computation.5 | loop fusion | flops 26209280 | bytes 21143552 | tf_op jit(solution)/shard_map/reduce_sum | solution.py:86
  63.6 3.3 %copy-done = f32[8,1024,128,5]{2,1,3,0:T(8,128)} copy-done((f32[8,1024,128,5]{2,1,3,0:T(8,128)}, f32[8,1024,128,5]{2,1,3,0:T(8,128)S(1)}, u32[]{:S(2)}) %copy-start) | copy-done | bytes 20971544
  66.9 10.3 %fusion.9 = bf16[128,8,5,128]{0,3,2,1:T(8,128)(2,1)S(1)} fusion(bf16[1024,8,128,1]{0,2,3,1:T(8,128)(2,1)S(1)} %bitcast.80, f32[8,1024,128,5]{2,1,3,0:T(8,128)} %copy-done, f32[128,8,5]{0,2,1:T(8,128)S(1)} %broadcast_maximum_fusion, pred[128,1024]{0,1:T(8,128)(4,1)S(1)} %fusion.12, f32[128,8,5]{0,2,1:T(8,128)S(1)} %fusion.1), kind=kOutput, calls=%fused_computation.16 | convolution fusion | flops 1369702400 | bytes 24551424 | tf_op jit(solution)/shard_map/qgrk,kgd->qgrd/dot_general | solution.py:87
  79.6 2.6 fusion.6
  83.6 14.6 %collective-permute-done = bf16[128,5120]{1,0:T(8,128)(2,1)S(1)} collective-permute-done((bf16[128,5120]{1,0:T(8,128)(2,1)S(1)}, bf16[128,5120]{1,0:T(8,128)(2,1)S(1)}, u32[]{:S(2)}, u32[]{:S(2)}) %collective-permute-start) | collective-permute-done | bytes 1310752 | tf_op jit(solution)/shard_map/ppermute | solution.py:27
  101.1 14.1 %collective-permute-done.1 = bf16[128,5120]{1,0:T(8,128)(2,1)S(1)} collective-permute-done((bf16[128,5120]{1,0:T(8,128)(2,1)S(1)}, bf16[128,5120]{1,0:T(8,128)(2,1)S(1)}, u32[]{:S(2)}, u32[]{:S(2)}) %collective-permute-start.1) | collective-permute-done | bytes 1310752 | tf_op jit(solution)/shard_map/ppermute | solution.py:27
  120.4 12.9 %collective-permute-done.2 = bf16[128,5120]{1,0:T(8,128)(2,1)} collective-permute-done((bf16[128,5120]{1,0:T(8,128)(2,1)S(1)}, bf16[128,5120]{1,0:T(8,128)(2,1)}, u32[]{:S(2)}, u32[]{:S(2)}) %collective-permute-start.2) | collective-permute-done | bytes 1310752 | tf_op jit(solution)/shard_map/ppermute | solution.py:27
  133.3 2.6 collective-permute-start.3
  138.8 11.9 %collective-permute-done.3 = bf16[128,5120]{1,0:T(8,128)(2,1)} collective-permute-done((bf16[128,5120]{1,0:T(8,128)(2,1)}, bf16[128,5120]{1,0:T(8,128)(2,1)}, u32[]{:S(2)}, u32[]{:S(2)}) %collective-permute-start.3) | collective-permute-done | bytes 1310752 | tf_op jit(solution)/shard_map/ppermute | solution.py:27
  153.2 2.6 bitcast_dynamic-update-slice_fusion.6
  165.7 9.6 %gather_fusion = bf16[8,128,5120]{2,1,0:T(8,128)(2,1)} fusion(bf16[8,128,5120]{2,1,0:T(8,128)(2,1)} %bitcast_dynamic-update-slice_fusion, s32[1024]{0:T(1024)S(1)} %pad_clamp_fusion), kind=kCustom, calls=%fused_computation | custom fusion | bytes 20971552 | tf_op jit(solution)/shard_map/gather | solution.py:32
  175.3 17.5 %fusion.21 = f32[1024,1024]{1,0:T(8,128)} fusion(bf16[1024,5120]{1,0:T(8,128)(2,1)} %bitcast.73, bf16[5120,1024]{0,1:T(8,128)(2,1)} %all-gather.7.cloned.1.call-done), kind=kOutput, calls=%fused_computation.50 | convolution fusion | flops 10737418240 | bytes 25165824 | tf_op jit(solution)/shard_map/dot_general | solution.py:129
  192.8 23.3 %all-gather.9.cloned.1.call-done = bf16[5120,1024]{0,1:T(8,128)(2,1)} async-done(((bf16[5120,64]{0,1:T(8,128)(2,1)}), bf16[5120,1024]{0,1:T(8,128)(2,1)}) %all-gather.9.cloned.1.call-update) | async-done | bytes 10485776 | tf_op jit(solution)/shard_map/all_gather | solution.py:126
  216.1 17.3 %multiply_convert_fusion = bf16[1024,1024]{1,0:T(8,128)(2,1)S(1)} fusion(f32[1024,1024]{1,0:T(8,128)} %fusion.21, bf16[1024,5120]{1,0:T(8,128)(2,1)} %bitcast.74, bf16[5120,1024]{0,1:T(8,128)(2,1)} %all-gather.9.cloned.1.call-done), kind=kOutput, calls=%fused_computation.9 | convolution fusion | flops 10743709696 | bytes 27262976 | tf_op jit(solution)/shard_map/dot_general | solution.py:130
  235.8 4.9 %all-to-all-start = ((bf16[8,128,1024]{1,2,0:T(8,128)(2,1)}), bf16[8,128,1024]{1,2,0:T(8,128)(2,1)S(1)}, u32[]{:S(2)}, u32[]{:S(2)}) async-start(bf16[8,128,1024]{1,2,0:T(8,128)(2,1)} %copy.56), calls=%async_computation | async-start | bytes 4194304 | tf_op jit(solution)/shard_map/all_to_all | solution.py:132
  240.9 6.5 %copy.58 = bf16[1024,2048]{1,0:T(8,128)(2,1)} copy(bf16[1024,2048]{0,1:T(8,128)(2,1)} %all-gather.5.cloned.1.call-done) | data formatting | bytes 8388608 | tf_op jit(solution)/shard_map/all_gather | solution.py:64
  247.4 7.5 %reshape.156 = bf16[64,32768]{1,0:T(8,128)(2,1)} reshape(bf16[1024,2048]{1,0:T(8,128)(2,1)} %copy.58) | data formatting | bytes 8388608 | tf_op jit(solution)/shard_map/reshape | solution.py:102
  254.8 2.9 %convolution_convert_fusion = bf16[16,32768]{1,0:T(8,128)(2,1)S(1)} fusion(bf16[64,32768]{1,0:T(8,128)(2,1)} %reshape.156, s32[64]{0:T(128)S(1)} %subtract_bitcast_fusion), kind=kOutput, calls=%fused_computation.1 | convolution fusion | flops 67634176 | bytes 5243136 | tf_op jit(solution)/shard_map/dot_general | solution.py:100
  259.5 7.6 %all-to-all-done = bf16[8,128,1024]{1,2,0:T(8,128)(2,1)S(1)} async-done(((bf16[8,128,1024]{1,2,0:T(8,128)(2,1)}), bf16[8,128,1024]{1,2,0:T(8,128)(2,1)S(1)}, u32[]{:S(2)}, u32[]{:S(2)}) %all-to-all-start) | async-done | bytes 2097184 | tf_op jit(solution)/shard_map/all_to_all | solution.py:132
  268.6 4.1 %copy.59 = bf16[128,8192]{1,0:T(8,128)(2,1)} copy(bf16[128,8192]{0,1:T(8,128)(2,1)} %bitcast.76) | data formatting | bytes 4194304
  (63 shorter events, 42.9 us)
Async XLA Ops:
  7.2 42.8 %all-gather.5.cloned.1.call-start = ((), (), s32[]{:S(2)}) async-start(), calls=%async_computation.1 | async-start | bytes 4718592 | tf_op jit(solution)/shard_map/all_gather | solution.py:64
  9.3 166.0 %all-gather.7.cloned.1.call-start = ((), (), s32[]{:S(2)}) async-start(), calls=%async_computation.2 | async-start | bytes 11141120 | tf_op jit(solution)/shard_map/all_gather | solution.py:125
  11.1 4.5 %copy-start.8 = (s32[1,128]{1,0:T(1,128)S(1)}, s32[1,128]{1,0:T(1,128)}, u32[]{:S(2)}) copy-start(s32[1,128]{1,0:T(1,128)} %param.11) | copy-start | bytes 1540
  11.1 16.3 %copy-start.3 = (bf16[128,5120]{1,0:T(8,128)(2,1)S(1)}, bf16[128,5120]{1,0:T(8,128)(2,1)}, u32[]{:S(2)}) copy-start(bf16[128,5120]{1,0:T(8,128)(2,1)} %param.9) | copy-start | bytes 3932164
  12.4 203.7 %all-gather.9.cloned.1.call-start = ((), (), s32[]{:S(2)}) async-start(), calls=%async_computation.3 | async-start | bytes 11141120 | tf_op jit(solution)/shard_map/all_gather | solution.py:126
  58.6 8.4 %copy-start = (f32[8,1024,128,5]{2,1,3,0:T(8,128)}, f32[8,1024,128,5]{2,1,3,0:T(8,128)S(1)}, u32[]{:S(2)}) copy-start(f32[8,1024,128,5]{2,1,3,0:T(8,128)S(1)} %get-tuple-element.20) | copy-start | bytes 62914564
  58.6 8.3 %copy-start.2 = (bf16[1024,1024]{0,1:T(8,128)(2,1)S(1)}, bf16[1024,1024]{0,1:T(8,128)(2,1)}, u32[]{:S(2)}) copy-start(bf16[1024,1024]{0,1:T(8,128)(2,1)} %get-tuple-element.18) | copy-start | bytes 6291460
  77.5 4.7 %copy-start.7 = (f32[5120]{0:T(1024)S(1)}, f32[5120]{0:T(1024)}, u32[]{:S(2)}) copy-start(f32[5120]{0:T(1024)} %param.13) | copy-start | bytes 61444
  82.2 75.9 %copy-start.1 = (bf16[128,5120]{1,0:T(8,128)(2,1)}, bf16[128,5120]{1,0:T(8,128)(2,1)S(1)}, u32[]{:S(2)}) copy-start(bf16[128,5120]{1,0:T(8,128)(2,1)S(1)} %get-tuple-element.16) | copy-start | bytes 3932164
  82.6 15.6 %collective-permute-start = (bf16[128,5120]{1,0:T(8,128)(2,1)S(1)}, bf16[128,5120]{1,0:T(8,128)(2,1)S(1)}, u32[]{:S(2)}, u32[]{:S(2)}) collective-permute-start(bf16[128,5120]{1,0:T(8,128)(2,1)S(1)} %fusion.8), channel_id=1, source_target_pairs={{0,1},{1,2},{2,3},{3,4},{4,5},{5,6},{6,7},{7,0},{8,9},{9,10},{10,1... | collective-permute-start | bytes 3932168 | tf_op jit(solution)/shard_map/ppermute | solution.py:27
  98.2 17.0 %collective-permute-start.1 = (bf16[128,5120]{1,0:T(8,128)(2,1)S(1)}, bf16[128,5120]{1,0:T(8,128)(2,1)S(1)}, u32[]{:S(2)}, u32[]{:S(2)}) collective-permute-start(bf16[128,5120]{1,0:T(8,128)(2,1)S(1)} %collective-permute-done), channel_id=1, source_target_pairs={{0,1},{1,2},{2,3},{3,4},{4,5},{5,6},{6,7},{7,0},{8,9},{9,10},{10,1... | collective-permute-start | bytes 3932168 | tf_op jit(solution)/shard_map/ppermute | solution.py:27
  100.6 18.1 %collective-permute-start.4 = (bf16[128,5120]{1,0:T(8,128)(2,1)S(1)}, bf16[128,5120]{1,0:T(8,128)(2,1)}, u32[]{:S(2)}, u32[]{:S(2)}) collective-permute-start(bf16[128,5120]{1,0:T(8,128)(2,1)S(1)} %fusion.8), channel_id=1, source_target_pairs={{1,0},{2,1},{3,2},{4,3},{5,4},{6,5},{7,6},{0,7},{9,8},{10,9},{11,1... | collective-permute-start | bytes 3932168 | tf_op jit(solution)/shard_map/ppermute | solution.py:29
  115.2 1.1 copy-start.4
  116.2 17.0 %collective-permute-start.2 = (bf16[128,5120]{1,0:T(8,128)(2,1)S(1)}, bf16[128,5120]{1,0:T(8,128)(2,1)}, u32[]{:S(2)}, u32[]{:S(2)}) collective-permute-start(bf16[128,5120]{1,0:T(8,128)(2,1)S(1)} %collective-permute-done.1), channel_id=1, source_target_pairs={{0,1},{1,2},{2,3},{3,4},{4,5},{5,6},{6,7},{7,0},{8,9},{9,10},{10,1... | collective-permute-start | bytes 3932168 | tf_op jit(solution)/shard_map/ppermute | solution.py:27
  118.7 17.6 %collective-permute-start.5 = (bf16[128,5120]{1,0:T(8,128)(2,1)}, bf16[128,5120]{1,0:T(8,128)(2,1)}, u32[]{:S(2)}, u32[]{:S(2)}) collective-permute-start(bf16[128,5120]{1,0:T(8,128)(2,1)} %collective-permute-done.4), channel_id=1, source_target_pairs={{1,0},{2,1},{3,2},{4,3},{5,4},{6,5},{7,6},{0,7},{9,8},{10,9},{11,1... | collective-permute-start | bytes 3932168 | tf_op jit(solution)/shard_map/ppermute | solution.py:29
  133.3 17.5 %collective-permute-start.3 = (bf16[128,5120]{1,0:T(8,128)(2,1)}, bf16[128,5120]{1,0:T(8,128)(2,1)}, u32[]{:S(2)}, u32[]{:S(2)}) collective-permute-start(bf16[128,5120]{1,0:T(8,128)(2,1)} %collective-permute-done.2), channel_id=1, source_target_pairs={{0,1},{1,2},{2,3},{3,4},{4,5},{5,6},{6,7},{7,0},{8,9},{9,10},{10,1... | collective-permute-start | bytes 3932168 | tf_op jit(solution)/shard_map/ppermute | solution.py:27
  135.9 19.9 %copy-start.5 = (bf16[128,5120]{1,0:T(8,128)(2,1)S(1)}, bf16[128,5120]{1,0:T(8,128)(2,1)}, u32[]{:S(2)}) copy-start(bf16[128,5120]{1,0:T(8,128)(2,1)} %copy-done.4) | copy-start | bytes 3932164
  136.4 28.1 %collective-permute-start.6 = (bf16[128,5120]{1,0:T(8,128)(2,1)}, bf16[128,5120]{1,0:T(8,128)(2,1)S(1)}, u32[]{:S(2)}, u32[]{:S(2)}) collective-permute-start(bf16[128,5120]{1,0:T(8,128)(2,1)} %collective-permute-done.5), channel_id=1, source_target_pairs={{1,0},{2,1},{3,2},{4,3},{5,4},{6,5},{7,6},{0,7},{9,8},{10,9},{11,1... | collective-permute-start | bytes 3932168 | tf_op jit(solution)/shard_map/ppermute | solution.py:29
  233.4 7.3 %copy-start.9 = (s32[1,128]{1,0:T(1,128)S(1)}, s32[1,128]{1,0:T(1,128)}, u32[]{:S(2)}) copy-start(s32[1,128]{1,0:T(1,128)} %param.17) | copy-start | bytes 1540
  235.8 31.3 %all-to-all-start = ((bf16[8,128,1024]{1,2,0:T(8,128)(2,1)}), bf16[8,128,1024]{1,2,0:T(8,128)(2,1)S(1)}, u32[]{:S(2)}, u32[]{:S(2)}) async-start(bf16[8,128,1024]{1,2,0:T(8,128)(2,1)} %copy.56), calls=%async_computation | async-start | bytes 4194304 | tf_op jit(solution)/shard_map/all_to_all | solution.py:132
  254.8 3.5 %copy-start.6 = (bf16[16,16,2048]{2,1,0:T(8,128)(2,1)S(1)}, bf16[16,16,2048]{2,1,0:T(8,128)(2,1)}, u32[]{:S(2)}) copy-start(bf16[16,16,2048]{2,1,0:T(8,128)(2,1)} %param.16) | copy-start | bytes 3145732
Sparse Core Ops, SparseCore 0:
  10.3 39.6 all-gather.4
  52.6 81.1 all-gather.6
  135.9 80.0 all-gather.8
